TPU v7x, 32 devices: a whole 2x2x4 slice. The times are simulated.
32 devices in a mesh: tm: 16 (over z, x, core), space: 2 (over y).
Axes of the slice: x: 2, y: 2, z: 4, core: 2. Of those that a mesh axis runs over, the one named last changes fastest.
Arguments:
- nodes: float32 [16, 2, 2, 8, 128, 128], P('tm', None, None, 'space'), may hold values from -3 to 3
- initial: float32 [2, 8, 128, 128], P(None, 'space'), may hold values from -3 to 3
Outputs:
- corrected: float32 [16, 2, 2, 8, 128, 128], P('tm', None, None, 'space')
All inputs are finite; a program needn't handle non-finite values.
Results may differ from a plain program's by a relative error of at most 0.0003.
Values sent between devices are 32-bit elements; how exact they have to be, the bound alone decides.
No kernel may reach another device: no remote copies, remote signals or barrier semaphores. Data moves between devices by JAX's collectives and lax.ppermute only.
A program may use at most 128 MiB of HBM per device.

v0:
```python
import math
import jax
import jax.numpy as jnp
from jax import lax
from jax.sharding import PartitionSpec as P

diffuse_fast = 0.5
diffuse_slow = 0.25
feed_rate = 0.04
kill_rate = 0.06
slice_length = 0.5
node_step = 0.25
sweep_weights = ((5.0 / 24.0, 1.0 / 3.0, -1.0 / 24.0), (-1.0 / 24.0, 1.0 / 3.0, 5.0 / 24.0))


def with_halo(x, sides, width):
    for axis, dim in sides:
        devices, length = (lax.axis_size(axis), x.shape[dim])
        up = [(i, (i + 1) % devices) for i in range(devices - 1)]
        down = [(j, i) for i, j in up]
        last = lax.slice_in_dim(x, length - width, length, axis=dim)
        leading = lax.slice_in_dim(x, 0, width, axis=dim)
        before = lax.ppermute(last, axis, up)
        after = lax.ppermute(leading, axis, down)
        x = jnp.concatenate([before, x, after], axis=dim)
    return x


def passed_along(value, axis, steps):
    count = lax.axis_size(axis)
    leading, last = (max(0, -steps), min(count, count - steps))
    return lax.ppermute(value, axis, [(source, source + steps) for source in range(leading, last)])


def entering(value, axis, join, neutral):
    count, mine = (lax.axis_size(axis), lax.axis_index(axis))
    pieces = jax.tree.map(lambda part: lax.all_gather(part, axis), value)
    subtotal = jax.tree.map(
        lambda part, zero: jnp.full_like(part, 0) + jnp.asarray(zero, part.dtype), value, neutral
    )

    def lap(position, subtotal):
        longer = join(subtotal, jax.tree.map(lambda part: part[position], pieces))
        return jax.tree.map(lambda new, old: jnp.where(position < mine, new, old), longer, subtotal)

    return lax.fori_loop(0, count - 1, lap, subtotal)


def sine_table(points, modes, stretch):
    place = jnp.arange(points).astype(jnp.float32) + 0.5
    order = jnp.arange(modes).astype(jnp.float32) + 1.0
    angle = math.pi / (stretch * modes) * place[:, None] * order[None, :]
    weight = jnp.where(jnp.arange(modes) == modes - 1, math.sqrt(0.5), 1.0).astype(jnp.float32)
    return math.sqrt(2.0 / modes) * weight[None, :] * jnp.sin(angle)


def tendency(values):
    center = values[..., 1:-1, :, :]
    padded = jnp.pad(center, [(0, 0)] * (center.ndim - 2) + [(1, 1), (1, 1)])
    laplace = (
        values[..., 2:, :, :]
        + values[..., :-2, :, :]
        + padded[..., 2:, 1:-1]
        + padded[..., :-2, 1:-1]
    )
    laplace = laplace + padded[..., 1:-1, 2:] + padded[..., 1:-1, :-2] - 6.0 * center
    first_kind = center[..., 0, :, :, :]
    second_kind = center[..., 1, :, :, :]
    reaction = (1.0 + first_kind) * second_kind * second_kind
    first_rate = diffuse_fast * laplace[..., 0, :, :, :] - reaction - feed_rate * first_kind
    second_rate = (
        diffuse_slow * laplace[..., 1, :, :, :] + reaction - (feed_rate + kill_rate) * second_kind
    )
    return jnp.stack([first_rate, second_rate], axis=-4)


def restrict(values):
    shape = values.shape
    blocks = values.reshape(shape[:-3] + (shape[-3] // 2, 2, shape[-2] // 2, 2, shape[-1] // 2, 2))
    return jnp.mean(blocks, axis=(-5, -3, -1))


def with_rims(values):
    return with_halo(values, (("space", 2),), 1)


def local(nodes, initial):
    planes_dev = initial.shape[1]
    width_x = initial.shape[2]
    width_y = initial.shape[3]
    spaces = lax.axis_size("space")
    modes_x = width_x // 2
    modes_y = width_y // 2
    modes_z = planes_dev * spaces // 2
    columns = modes_x * modes_y // spaces
    highest = lax.Precision.HIGHEST
    (w00, w01, w02), (w10, w11, w12) = sweep_weights
    own_nodes = nodes[0]
    prior_end = passed_along(own_nodes[1], "tm", 1)
    is_first = lax.axis_index("tm") == 0
    start_value = jnp.where(is_first, initial, prior_end)
    stacked = jnp.stack([start_value, own_nodes[0], own_nodes[1]])
    slopes = tendency(with_rims(stacked))
    swept_one = start_value + slice_length * (w00 * slopes[0] + w01 * slopes[1] + w02 * slopes[2])
    slope_one = tendency(with_rims(swept_one[None]))[0]
    swept_two = (
        swept_one
        + node_step * (slope_one - slopes[1])
        + slice_length * (w10 * slopes[0] + w11 * slopes[1] + w12 * slopes[2])
    )
    slope_two = tendency(with_rims(swept_two[None]))[0]
    integral_one = slice_length * (w00 * slopes[0] + w01 * slope_one + w02 * slope_two)
    integral_two = slice_length * (w10 * slopes[0] + w11 * slope_one + w12 * slope_two)
    coarse = restrict(jnp.stack([integral_one, integral_two, start_value, swept_one, swept_two]))
    forward_x = sine_table(modes_x, modes_x, 1.0).T
    forward_y = sine_table(modes_y, modes_y, 1.0).T
    forward_z = sine_table(modes_z, modes_z, 1.0).T
    along_y = jnp.einsum("by,fszxy->fszxb", forward_y, coarse, precision=highest)
    spectra_xy = jnp.einsum("ax,fszxb->fszab", forward_x, along_y, precision=highest)
    spectra_xy = spectra_xy.reshape(5, 2, planes_dev // 2, modes_x * modes_y)
    gathered = lax.all_to_all(spectra_xy, "space", split_axis=3, concat_axis=2, tiled=True)
    spectra = jnp.einsum("kz,fszc->fskc", forward_z, gathered, precision=highest)
    column_ids = lax.axis_index("space") * columns + jnp.arange(columns)
    order_x = (column_ids // modes_y + 1).astype(jnp.float32)
    order_y = (column_ids % modes_y + 1).astype(jnp.float32)
    order_z = jnp.arange(modes_z).astype(jnp.float32) + 1.0
    eigen_xy = (
        2.0 * jnp.cos(math.pi * order_x / modes_x)
        - 2.0
        + 2.0 * jnp.cos(math.pi * order_y / modes_y)
        - 2.0
    )
    eigen_z = 2.0 * jnp.cos(math.pi * order_z / modes_z) - 2.0
    eigen_sum = (eigen_z[:, None] + eigen_xy[None, :]) / 4.0
    linear = jnp.stack(
        [diffuse_fast * eigen_sum - feed_rate, diffuse_slow * eigen_sum - (feed_rate + kill_rate)]
    )
    factor = 1.0 / (1.0 - node_step * linear)
    remain_one = spectra[0] - node_step * linear * spectra[3]
    remain_two = spectra[1] - node_step * linear * spectra[4]
    seed_value = jnp.where(is_first, spectra[2], 0.0)
    element = factor * (factor * (seed_value + remain_one) + remain_two)
    log_gain = 2.0 * jnp.log(factor)

    def join_counts(earlier, later):
        return (earlier[0] + later[0], jnp.exp(later[0] * log_gain) * earlier[1] + later[1])

    _, prefix = entering(
        (jnp.ones((), jnp.float32), element),
        "tm",
        join_counts,
        (jnp.zeros((), jnp.float32), jnp.zeros_like(element)),
    )
    start_hat = jnp.where(is_first, spectra[2], prefix)
    new_one = factor * (start_hat + remain_one)
    new_two = factor * (new_one + remain_two)
    change = jnp.stack([new_one - spectra[3], new_two - spectra[4]])
    interp_x = sine_table(width_x, modes_x, 2.0)
    interp_y = sine_table(width_y, modes_y, 2.0)
    interp_z = sine_table(planes_dev * spaces, modes_z, 2.0)
    at_planes = jnp.einsum("zk,fskc->fszc", interp_z, change, precision=highest)
    returned = lax.all_to_all(at_planes, "space", split_axis=2, concat_axis=3, tiled=True)
    returned = returned.reshape(2, 2, planes_dev, modes_x, modes_y)
    widened_y = jnp.einsum("yb,fszab->fszay", interp_y, returned, precision=highest)
    refined = jnp.einsum("xa,fszay->fszxy", interp_x, widened_y, precision=highest)
    corrected = jnp.stack([swept_one + refined[0], swept_two + refined[1]])
    return corrected[None]


def solution(mesh):
    in_specs = (P("tm", None, None, "space", None, None), P(None, "space", None, None))
    out_specs = P("tm", None, None, "space", None, None)
    return jax.shard_map(local, mesh=mesh, in_specs=in_specs, out_specs=out_specs, check_vma=False)
```

profile of v0, /device:TPU:0, one launch (start us, length us, event | category | flops | bytes accessed | tf_op | source)
XLA Modules:
  0.0 521.1 jit_solution(6361830666859375832)
XLA Ops:
  8.1 3.2 collective-permute-start
  14.4 6.0 %collective-permute-start.2 = (f32[3,2,1,128,128]{3,4,2,1,0:T(8,128)S(1)}, f32[3,2,1,128,128]{3,4,2,1,0:T(8,128)}, u32[]{:S(2)}, u32[]{:S(2)}) collective-permute-start(f32[3,2,1,128,128]{3,4,2,1,0:T(8,128)S(1)} %get-tuple-element.157), channel_id=1, source_target_pairs={{0,1},{2,3},{4,5},{6,7},{8,9},{10,11},{12,13},{14,15},{16,17},{18,... | collective-permute-start | bytes 1179656 | tf_op jit(solution)/shard_map/ppermute | solution.py:23
  20.6 2.5 collective-permute-done.1
  25.0 2.0 fusion.5
  28.9 4.6 collective-permute-start.4
  38.6 4.8 collective-permute-start.6
  43.5 34.9 %reshape.454 = f32[1,2,2,2,64,2,64,2]{5,4,7,6,3,2,1,0:T(8,128)} reshape(f32[2,4,128,128]{2,3,1,0:T(8,128)S(1)} %broadcast_select_fusion) | data formatting | bytes 1048576 | tf_op jit(solution)/shard_map/stack | solution.py:114
  78.4 22.8 %copy.49 = f32[1,2,2,2,64,2,64,2]{6,4,7,5,3,2,1,0:T(8,128)S(1)} copy(f32[1,2,2,2,64,2,64,2]{5,4,7,6,3,2,1,0:T(8,128)} %reshape.454) | data formatting | bytes 1048576 | tf_op jit(solution)/shard_map/stack | solution.py:114
  101.2 34.8 %reshape.455 = f32[1,2,2,2,64,2,64,2]{5,4,7,6,3,2,1,0:T(8,128)} reshape(f32[2,4,128,128]{2,3,1,0:T(8,128)S(1)} %get-tuple-element.150) | data formatting | bytes 1048576 | tf_op jit(solution)/shard_map/stack | solution.py:114
  136.0 23.8 %copy.50 = f32[1,2,2,2,64,2,64,2]{6,4,7,5,3,2,1,0:T(8,128)} copy(f32[1,2,2,2,64,2,64,2]{5,4,7,6,3,2,1,0:T(8,128)} %reshape.455) | data formatting | bytes 1048576 | tf_op jit(solution)/shard_map/stack | solution.py:114
  159.8 34.8 %reshape.456 = f32[1,2,2,2,64,2,64,2]{5,4,7,6,3,2,1,0:T(8,128)} reshape(f32[2,4,128,128]{2,3,1,0:T(8,128)S(1)} %bitcast_add_fusion.1) | data formatting | bytes 1048576 | tf_op jit(solution)/shard_map/stack | solution.py:114
  194.6 23.8 %copy.51 = f32[1,2,2,2,64,2,64,2]{6,4,7,5,3,2,1,0:T(8,128)} copy(f32[1,2,2,2,64,2,64,2]{5,4,7,6,3,2,1,0:T(8,128)} %reshape.456) | data formatting | bytes 1048576 | tf_op jit(solution)/shard_map/stack | solution.py:114
  220.1 35.6 %reshape.452 = f32[1,2,2,2,64,2,64,2]{5,4,7,6,3,2,1,0:T(8,128)} reshape(f32[1,2,4,128,128]{3,4,2,1,0:T(8,128)} %get-tuple-element.155) | data formatting | bytes 1048576 | tf_op jit(solution)/shard_map/stack | solution.py:114
  255.7 23.8 %copy.47 = f32[1,2,2,2,64,2,64,2]{6,4,7,5,3,2,1,0:T(8,128)} copy(f32[1,2,2,2,64,2,64,2]{5,4,7,6,3,2,1,0:T(8,128)} %reshape.452) | data formatting | bytes 1048576 | tf_op jit(solution)/shard_map/stack | solution.py:114
  279.4 2.4 constant_dynamic-update-slice_fusion.4
  281.8 34.8 %reshape.453 = f32[1,2,2,2,64,2,64,2]{5,4,7,6,3,2,1,0:T(8,128)} reshape(f32[1,2,4,128,128]{3,4,2,1,0:T(8,128)S(1)} %copy-done.2) | data formatting | bytes 1048576 | tf_op jit(solution)/shard_map/stack | solution.py:114
  316.7 24.3 %copy.48 = f32[1,2,2,2,64,2,64,2]{6,4,7,5,3,2,1,0:T(8,128)} copy(f32[1,2,2,2,64,2,64,2]{5,4,7,6,3,2,1,0:T(8,128)} %reshape.453) | data formatting | bytes 1048576 | tf_op jit(solution)/shard_map/stack | solution.py:114
  341.0 2.3 constant_dynamic-update-slice_fusion.3
  347.6 3.2 reduce_sum.9
  350.8 2.2 fusion.11
  353.8 9.3 %copy.74 = f32[5,2,2,64,64]{0,2,1,4,3:T(2,128)} copy(f32[5,2,2,64,64]{3,4,2,1,0:T(8,128)S(1)} %convolution_bitcast_fusion.3) | data formatting | bytes 655360 | tf_op jit(solution)/shard_map/reshape | solution.py:120
  363.1 15.4 %reshape.457 = f32[2,1,40960]{2,1,0:T(1,128)} reshape(f32[4096,2,2,5]{3,2,1,0:T(2,128)} %bitcast.154) | data formatting | bytes 655360
  378.5 3.5 all-to-all-start
  382.2 5.3 %all-to-all-done = f32[2,1,40960]{2,1,0:T(1,128)S(1)} async-done(((f32[2,1,40960]{2,1,0:T(1,128)}), f32[2,1,40960]{2,1,0:T(1,128)S(1)}, u32[]{:S(2)}, u32[]{:S(2)}) %all-to-all-start) | async-done | bytes 327712 | tf_op jit(solution)/shard_map/all_to_all | solution.py:121
  389.7 15.5 %reshape.458 = f32[4096,2,2,5]{3,2,1,0:T(2,128)} reshape(f32[2,40960]{1,0:T(2,128)S(1)} %reduce) | data formatting | bytes 655360
  405.1 10.3 %copy.55 = f32[5,2,2,2,2048]{4,2,3,1,0:T(2,128)S(1)} copy(f32[5,2,2,2,2048]{0,2,1,4,3:T(2,128)} %bitcast.155) | data formatting | bytes 655360 | tf_op jit(solution)/shard_map/all_to_all | solution.py:121
  418.6 39.5 %all-reduce.3 = f32[16]{0:T(128)S(1)} all-reduce(f32[16]{0:T(128)S(1)} %dynamic-update-slice), channel_id=1, replica_groups=mesh['tm'=16,'space'=2] {'tm'}, use_global_device_ids=true, to_apply=%add.3 | all-reduce | flops 16 | bytes 128
  458.1 7.7 %all-gather.2.cloned.1.call-done = f32[16,2,4,2048]{3,2,1,0:T(4,128)} async-done(((f32[1,2,4,2048]{3,2,1,0:T(4,128)}), f32[16,2,4,2048]{3,2,1,0:T(4,128)}) %all-gather.2.cloned.1.call-update) | async-done | bytes 1048592 | tf_op jit(solution)/shard_map/all_gather | solution.py:37
  465.8 32.5 %while.14 = (s32[]{:T(128)}, f32[2,4,2048]{2,1,0:T(4,128)S(1)}, s32[]{:T(128)}, f32[16]{0:T(128)S(1)}, f32[2,4,2048]{2,1,0:T(4,128)S(1)}, /*index=5*/f32[16,2,4,2048]{3,2,1,0:T(4,128)}, s32[]{:T(128)}, s32[]{:T(128)}) while((s32[]{:T(128)}, f32[2,4,2048]{2,1,0:T(4,128)S(1)}, s32[]{:T(128)}, f32[16]{0:T(128)S(1)}, ...), condition=%wide.region_2.3_spmd.clone, body=%wide.region_1.2_spmd.clone.sunk | while | flops 81924 | bytes 262269 | solution.py:46
  499.9 3.7 all-to-all-start.1
  503.6 5.8 %all-to-all-done.1 = f32[2,2,8,2048]{3,1,0,2:T(2,128)S(1)} async-done(((f32[2,2,8,2048]{3,1,0,2:T(2,128)}), f32[2,2,8,2048]{3,1,0,2:T(2,128)S(1)}, u32[]{:S(2)}, u32[]{:S(2)}) %all-to-all-start.1) | async-done | bytes 262176 | tf_op jit(solution)/shard_map/all_to_all | solution.py:162
  510.7 1.9 convolution_bitcast_fusion.2
  (101 shorter events, 62.7 us)
Async XLA Ops:
  6.5 4.8 copy-start.3
  8.1 4.1 collective-permute-start
  13.2 10.0 %collective-permute-start.1 = (f32[3,2,1,128,128]{3,4,2,1,0:T(8,128)}, f32[3,2,1,128,128]{3,4,2,1,0:T(8,128)}, u32[]{:S(2)}, u32[]{:S(2)}) collective-permute-start(f32[3,2,1,128,128]{3,4,2,1,0:T(8,128)} %get-tuple-element.156), channel_id=1, source_target_pairs={{1,0},{3,2},{5,4},{7,6},{9,8},{11,10},{13,12},{15,14},{17,16},{19,... | collective-permute-start | bytes 1179656 | tf_op jit(solution)/shard_map/ppermute | solution.py:24
  14.4 10.6 %collective-permute-start.2 = (f32[3,2,1,128,128]{3,4,2,1,0:T(8,128)S(1)}, f32[3,2,1,128,128]{3,4,2,1,0:T(8,128)}, u32[]{:S(2)}, u32[]{:S(2)}) collective-permute-start(f32[3,2,1,128,128]{3,4,2,1,0:T(8,128)S(1)} %get-tuple-element.157), channel_id=1, source_target_pairs={{0,1},{2,3},{4,5},{6,7},{8,9},{10,11},{12,13},{14,15},{16,17},{18,... | collective-permute-start | bytes 1179656 | tf_op jit(solution)/shard_map/ppermute | solution.py:23
  27.6 6.9 %collective-permute-start.3 = (f32[1,2,1,128,128]{3,4,2,1,0:T(8,128)S(1)}, f32[1,2,1,128,128]{3,4,2,1,0:T(8,128)S(1)}, u32[]{:S(2)}, u32[]{:S(2)}) collective-permute-start(f32[1,2,1,128,128]{3,4,2,1,0:T(8,128)S(1)} %get-tuple-element.168), channel_id=1, source_target_pairs={{1,0},{3,2},{5,4},{7,6},{9,8},{11,10},{13,12},{15,14},{17,16},{19,... | collective-permute-start | bytes 393224 | tf_op jit(solution)/shard_map/ppermute | solution.py:24
  28.9 7.1 %collective-permute-start.4 = (f32[1,2,1,128,128]{3,4,2,1,0:T(8,128)S(1)}, f32[1,2,1,128,128]{3,4,2,1,0:T(8,128)S(1)}, u32[]{:S(2)}, u32[]{:S(2)}) collective-permute-start(f32[1,2,1,128,128]{3,4,2,1,0:T(8,128)S(1)} %get-tuple-element.169), channel_id=1, source_target_pairs={{0,1},{2,3},{4,5},{6,7},{8,9},{10,11},{12,13},{14,15},{16,17},{18,... | collective-permute-start | bytes 393224 | tf_op jit(solution)/shard_map/ppermute | solution.py:23
  37.3 181.1 %collective-permute-start.5 = (f32[1,2,1,128,128]{3,4,2,1,0:T(8,128)}, f32[1,2,1,128,128]{3,4,2,1,0:T(8,128)S(1)}, u32[]{:S(2)}, u32[]{:S(2)}) collective-permute-start(f32[1,2,1,128,128]{3,4,2,1,0:T(8,128)} %get-tuple-element.166), channel_id=1, source_target_pairs={{1,0},{3,2},{5,4},{7,6},{9,8},{11,10},{13,12},{15,14},{17,16},{19,... | collective-permute-start | bytes 393224 | tf_op jit(solution)/shard_map/ppermute | solution.py:24
  38.6 179.8 %collective-permute-start.6 = (f32[1,2,1,128,128]{3,4,2,1,0:T(8,128)}, f32[1,2,1,128,128]{3,4,2,1,0:T(8,128)S(1)}, u32[]{:S(2)}, u32[]{:S(2)}) collective-permute-start(f32[1,2,1,128,128]{3,4,2,1,0:T(8,128)} %get-tuple-element.167), channel_id=1, source_target_pairs={{0,1},{2,3},{4,5},{6,7},{8,9},{10,11},{12,13},{14,15},{16,17},{18,... | collective-permute-start | bytes 393224 | tf_op jit(solution)/shard_map/ppermute | solution.py:23
  279.4 2.4 copy-start.2
  343.3 1.6 copy-start
  344.9 1.6 copy-start.1
  378.5 9.0 %all-to-all-start = ((f32[2,1,40960]{2,1,0:T(1,128)}), f32[2,1,40960]{2,1,0:T(1,128)S(1)}, u32[]{:S(2)}, u32[]{:S(2)}) async-start(f32[2,1,40960]{2,1,0:T(1,128)} %reshape.457), calls=%async_computation | async-start | bytes 655360 | tf_op jit(solution)/shard_map/all_to_all | solution.py:121
  382.0 83.8 %all-gather.2.cloned.1.call-start = ((), (), s32[]{:S(2)}) async-start(), calls=%async_computation.2 | async-start | bytes 1114112 | tf_op jit(solution)/shard_map/all_gather | solution.py:37
  415.4 1.8 copy-start.4
  499.9 9.5 %all-to-all-start.1 = ((f32[2,2,8,2048]{3,1,0,2:T(2,128)}), f32[2,2,8,2048]{3,1,0,2:T(2,128)S(1)}, u32[]{:S(2)}, u32[]{:S(2)}) async-start(f32[2,2,8,2048]{3,1,0,2:T(2,128)} %copy.56), calls=%async_computation.1 | async-start | bytes 524288 | tf_op jit(solution)/shard_map/all_to_all | solution.py:162
Sparse Core Ops, SparseCore 0:
  417.4 48.3 all-gather.1
where the time goes:
time: 528 us; the launch traced here: 521 us
  local copies, waits for them, and re-layouts  370 us (70%)
  blocking collectives  39.5 us (7%)
  other arithmetic  34.8 us (7%)
  starting transfers between devices  29.8 us (6%)
  waiting for transfers between devices  26 us (5%)
  between operations  14 us (3%)
  matrix products  6.93 us (1%)
    another operation x11, local copies, waits for them, and re-layouts, local(): jnp.stack([integral_one, integral_two, start_value, swept_one, swept_two])  295 us
    unnamed x22, local copies, waits for them, and re-layouts  40.7 us
    unnamed x1, blocking collectives  39.5 us
    select_n x15, other arithmetic, lap(): jnp.where(position < mine, new, old)  23.6 us
    ppermute x3, starting transfers between devices, with_halo(): before = lax.ppermute(last, axis, up)  15.4 us
    all_to_all x3, local copies, waits for them, and re-layouts, local(): lax.all_to_all(spectra_xy, 'space', split_axis=3, concat_axis=2, tiled=True)  11.1 us
  transfers between devices with their start and end apart: 10, of which 8 were waited for; matrix products, arithmetic and copies ran while one was open for 34% of the time, Pallas kernels for 0%

commit v1 on v0

--- a/solution.py
+++ b/solution.py
@@ -118,7 +118,12 @@
     along_y = jnp.einsum("by,fszxy->fszxb", forward_y, coarse, precision=highest)
     spectra_xy = jnp.einsum("ax,fszxb->fszab", forward_x, along_y, precision=highest)
     spectra_xy = spectra_xy.reshape(5, 2, planes_dev // 2, modes_x * modes_y)
-    gathered = lax.all_to_all(spectra_xy, "space", split_axis=3, concat_axis=2, tiled=True)
+    gathered = jnp.concatenate(
+        lax.all_to_all(
+            jnp.stack(jnp.split(spectra_xy, lax.axis_size("space"), axis=3)), "space", 0, 0
+        ),
+        axis=2,
+    )
     spectra = jnp.einsum("kz,fszc->fskc", forward_z, gathered, precision=highest)
     column_ids = lax.axis_index("space") * columns + jnp.arange(columns)
     order_x = (column_ids // modes_y + 1).astype(jnp.float32)

time: 528 us -> 472 us (0.89)
  local copies, waits for them, and re-layouts: 370 us -> 319 us
    unnamed x22 -> x20, local copies, waits for them, and re-layouts: 40.7 us -> 9.74 us
    all_to_all x3 -> x0, local copies, waits for them, and re-layouts: 11.1 us -> none  [local(): lax.all_to_all(spectra_xy, 'space', split_axis=3, concat_axis=2, tiled=True)]
    reshape x1, local copies, waits for them, and re-layouts: 9.27 us -> 0.34 us  [local(): spectra_xy = spectra_xy.reshape(5, 2, planes_dev // 2, modes_x * modes_y)]
  transfers between devices with their start and end apart: 10 -> 10, of which waited for: 8 -> 8; matrix products, arithmetic and copies ran while one was open for 34% -> 38% of each run, Pallas kernels for 0% -> 0%
where the time goes in v1:
time: 472 us; the launch traced here: 469 us
  local copies, waits for them, and re-layouts  319 us (68%)
  blocking collectives  39.5 us (8%)
  other arithmetic  34 us (7%)
  starting transfers between devices  29.5 us (6%)
  waiting for transfers between devices  26.2 us (6%)
  between operations  13.7 us (3%)
  matrix products  6.93 us (1%)
    another operation x11, local copies, waits for them, and re-layouts, local(): jnp.stack([integral_one, integral_two, start_value, swept_one, swept_two])  294 us
    unnamed x1, blocking collectives  39.5 us
    select_n x15, other arithmetic, lap(): jnp.where(position < mine, new, old)  23.6 us
    ppermute x3, starting transfers between devices, with_halo(): before = lax.ppermute(last, axis, up)  15.3 us
    unnamed x20, local copies, waits for them, and re-layouts  9.74 us
  transfers between devices with their start and end apart: 10, of which 8 were waited for; matrix products, arithmetic and copies ran while one was open for 38% of the time, Pallas kernels for 0%

profile of v1, /device:TPU:0, one launch (start us, length us, event | category | flops | bytes accessed | tf_op | source)
XLA Modules:
  0.0 469.1 jit_solution(58851464985563142)
XLA Ops:
  8.1 3.2 collective-permute-start
  14.4 6.0 %collective-permute-start.2 = (f32[3,2,1,128,128]{3,4,2,1,0:T(8,128)S(1)}, f32[3,2,1,128,128]{3,4,2,1,0:T(8,128)}, u32[]{:S(2)}, u32[]{:S(2)}) collective-permute-start(f32[3,2,1,128,128]{3,4,2,1,0:T(8,128)S(1)} %get-tuple-element.157), channel_id=1, source_target_pairs={{0,1},{2,3},{4,5},{6,7},{8,9},{10,11},{12,13},{14,15},{16,17},{18,... | collective-permute-start | bytes 1179656 | tf_op jit(solution)/shard_map/ppermute | solution.py:23
  20.6 2.5 collective-permute-done.1
  23.1 1.9 collective-permute-done.2
  25.0 2.0 fusion.5
  28.9 4.6 collective-permute-start.4
  38.7 4.7 %collective-permute-start.6 = (f32[1,2,1,128,128]{3,4,2,1,0:T(8,128)}, f32[1,2,1,128,128]{3,4,2,1,0:T(8,128)S(1)}, u32[]{:S(2)}, u32[]{:S(2)}) collective-permute-start(f32[1,2,1,128,128]{3,4,2,1,0:T(8,128)} %get-tuple-element.167), channel_id=1, source_target_pairs={{0,1},{2,3},{4,5},{6,7},{8,9},{10,11},{12,13},{14,15},{16,17},{18,... | collective-permute-start | bytes 393224 | tf_op jit(solution)/shard_map/ppermute | solution.py:23
  43.4 34.9 %reshape.462 = f32[1,2,2,2,64,2,64,2]{5,4,7,6,3,2,1,0:T(8,128)} reshape(f32[2,4,128,128]{2,3,1,0:T(8,128)S(1)} %broadcast_select_fusion) | data formatting | bytes 1048576 | tf_op jit(solution)/shard_map/stack | solution.py:114
  78.3 22.8 %copy.30 = f32[1,2,2,2,64,2,64,2]{6,4,7,5,3,2,1,0:T(8,128)S(1)} copy(f32[1,2,2,2,64,2,64,2]{5,4,7,6,3,2,1,0:T(8,128)} %reshape.462) | data formatting | bytes 1048576 | tf_op jit(solution)/shard_map/stack | solution.py:114
  101.1 34.9 %reshape.463 = f32[1,2,2,2,64,2,64,2]{5,4,7,6,3,2,1,0:T(8,128)} reshape(f32[2,4,128,128]{2,3,1,0:T(8,128)S(1)} %get-tuple-element.150) | data formatting | bytes 1048576 | tf_op jit(solution)/shard_map/stack | solution.py:114
  136.0 23.8 %copy.31 = f32[1,2,2,2,64,2,64,2]{6,4,7,5,3,2,1,0:T(8,128)} copy(f32[1,2,2,2,64,2,64,2]{5,4,7,6,3,2,1,0:T(8,128)} %reshape.463) | data formatting | bytes 1048576 | tf_op jit(solution)/shard_map/stack | solution.py:114
  159.7 34.8 %reshape.464 = f32[1,2,2,2,64,2,64,2]{5,4,7,6,3,2,1,0:T(8,128)} reshape(f32[2,4,128,128]{2,3,1,0:T(8,128)S(1)} %bitcast_add_fusion.1) | data formatting | bytes 1048576 | tf_op jit(solution)/shard_map/stack | solution.py:114
  194.6 23.8 %copy.32 = f32[1,2,2,2,64,2,64,2]{6,4,7,5,3,2,1,0:T(8,128)} copy(f32[1,2,2,2,64,2,64,2]{5,4,7,6,3,2,1,0:T(8,128)} %reshape.464) | data formatting | bytes 1048576 | tf_op jit(solution)/shard_map/stack | solution.py:114
  220.0 35.6 %reshape.460 = f32[1,2,2,2,64,2,64,2]{5,4,7,6,3,2,1,0:T(8,128)} reshape(f32[1,2,4,128,128]{3,4,2,1,0:T(8,128)} %get-tuple-element.155) | data formatting | bytes 1048576 | tf_op jit(solution)/shard_map/stack | solution.py:114
  255.6 23.8 %copy.28 = f32[1,2,2,2,64,2,64,2]{6,4,7,5,3,2,1,0:T(8,128)} copy(f32[1,2,2,2,64,2,64,2]{5,4,7,6,3,2,1,0:T(8,128)} %reshape.460) | data formatting | bytes 1048576 | tf_op jit(solution)/shard_map/stack | solution.py:114
  279.4 2.4 constant_dynamic-update-slice_fusion.4
  281.7 34.8 %reshape.461 = f32[1,2,2,2,64,2,64,2]{5,4,7,6,3,2,1,0:T(8,128)} reshape(f32[1,2,4,128,128]{3,4,2,1,0:T(8,128)S(1)} %copy-done.2) | data formatting | bytes 1048576 | tf_op jit(solution)/shard_map/stack | solution.py:114
  316.6 23.8 %copy.29 = f32[1,2,2,2,64,2,64,2]{6,4,7,5,3,2,1,0:T(8,128)} copy(f32[1,2,2,2,64,2,64,2]{5,4,7,6,3,2,1,0:T(8,128)} %reshape.461) | data formatting | bytes 1048576 | tf_op jit(solution)/shard_map/stack | solution.py:114
  340.4 2.3 constant_dynamic-update-slice_fusion.3
  347.0 3.2 reduce_sum.9
  350.2 2.2 fusion.11
  354.7 3.6 all-to-all-start
  358.4 5.4 %all-to-all-done = f32[2,5,2,2,2048]{4,3,2,1,0:T(2,128)S(1)} async-done(((f32[2,5,2,2,2048]{4,3,2,1,0:T(2,128)}), f32[2,5,2,2,2048]{4,3,2,1,0:T(2,128)S(1)}, u32[]{:S(2)}, u32[]{:S(2)}) %all-to-all-start) | async-done | bytes 327712 | tf_op jit(solution)/shard_map/all_to_all | solution.py:122
  366.9 39.5 %all-reduce.3 = f32[16]{0:T(128)S(1)} all-reduce(f32[16]{0:T(128)S(1)} %dynamic-update-slice), channel_id=1, replica_groups=mesh['tm'=16,'space'=2] {'tm'}, use_global_device_ids=true, to_apply=%add.3 | all-reduce | flops 16 | bytes 128
  406.5 7.7 %all-gather.2.cloned.1.call-done = f32[16,2,4,2048]{3,2,1,0:T(4,128)} async-done(((f32[1,2,4,2048]{3,2,1,0:T(4,128)}), f32[16,2,4,2048]{3,2,1,0:T(4,128)}) %all-gather.2.cloned.1.call-update) | async-done | bytes 1048592 | tf_op jit(solution)/shard_map/all_gather | solution.py:37
  414.2 32.5 %while.14 = (s32[]{:T(128)}, f32[2,4,2048]{2,1,0:T(4,128)S(1)}, s32[]{:T(128)}, f32[16]{0:T(128)S(1)}, f32[2,4,2048]{2,1,0:T(4,128)S(1)}, /*index=5*/f32[16,2,4,2048]{3,2,1,0:T(4,128)}, s32[]{:T(128)}, s32[]{:T(128)}) while((s32[]{:T(128)}, f32[2,4,2048]{2,1,0:T(4,128)S(1)}, s32[]{:T(128)}, f32[16]{0:T(128)S(1)}, ...), condition=%wide.region_2.3_spmd.clone, body=%wide.region_1.2_spmd.clone.sunk | while | flops 81924 | bytes 262269 | solution.py:46
  414.8 1.6 fusion.119
  419.1 1.6 fusion.119
  421.3 1.6 fusion.119
  448.3 3.4 all-to-all-start.1
  451.7 5.8 %all-to-all-done.1 = f32[2,2,8,2048]{3,1,0,2:T(2,128)S(1)} async-done(((f32[2,2,8,2048]{3,1,0,2:T(2,128)}), f32[2,2,8,2048]{3,1,0,2:T(2,128)S(1)}, u32[]{:S(2)}, u32[]{:S(2)}) %all-to-all-start.1) | async-done | bytes 262176 | tf_op jit(solution)/shard_map/all_to_all | solution.py:167
  458.8 1.9 convolution_bitcast_fusion.2
  (100 shorter events, 55.3 us)
Async XLA Ops:
  6.5 4.8 %copy-start.3 = (f32[2,4,128,128]{3,2,1,0:T(8,128)S(1)}, f32[2,4,128,128]{3,2,1,0:T(8,128)}, u32[]{:S(2)}) copy-start(f32[2,4,128,128]{3,2,1,0:T(8,128)} %param.5) | copy-start | bytes 1572868
  8.1 4.1 collective-permute-start
  13.2 10.0 %collective-permute-start.1 = (f32[3,2,1,128,128]{3,4,2,1,0:T(8,128)}, f32[3,2,1,128,128]{3,4,2,1,0:T(8,128)}, u32[]{:S(2)}, u32[]{:S(2)}) collective-permute-start(f32[3,2,1,128,128]{3,4,2,1,0:T(8,128)} %get-tuple-element.156), channel_id=1, source_target_pairs={{1,0},{3,2},{5,4},{7,6},{9,8},{11,10},{13,12},{15,14},{17,16},{19,... | collective-permute-start | bytes 1179656 | tf_op jit(solution)/shard_map/ppermute | solution.py:24
  14.4 10.6 %collective-permute-start.2 = (f32[3,2,1,128,128]{3,4,2,1,0:T(8,128)S(1)}, f32[3,2,1,128,128]{3,4,2,1,0:T(8,128)}, u32[]{:S(2)}, u32[]{:S(2)}) collective-permute-start(f32[3,2,1,128,128]{3,4,2,1,0:T(8,128)S(1)} %get-tuple-element.157), channel_id=1, source_target_pairs={{0,1},{2,3},{4,5},{6,7},{8,9},{10,11},{12,13},{14,15},{16,17},{18,... | collective-permute-start | bytes 1179656 | tf_op jit(solution)/shard_map/ppermute | solution.py:23
  27.6 6.9 %collective-permute-start.3 = (f32[1,2,1,128,128]{3,4,2,1,0:T(8,128)S(1)}, f32[1,2,1,128,128]{3,4,2,1,0:T(8,128)S(1)}, u32[]{:S(2)}, u32[]{:S(2)}) collective-permute-start(f32[1,2,1,128,128]{3,4,2,1,0:T(8,128)S(1)} %get-tuple-element.168), channel_id=1, source_target_pairs={{1,0},{3,2},{5,4},{7,6},{9,8},{11,10},{13,12},{15,14},{17,16},{19,... | collective-permute-start | bytes 393224 | tf_op jit(solution)/shard_map/ppermute | solution.py:24
  28.9 7.1 %collective-permute-start.4 = (f32[1,2,1,128,128]{3,4,2,1,0:T(8,128)S(1)}, f32[1,2,1,128,128]{3,4,2,1,0:T(8,128)S(1)}, u32[]{:S(2)}, u32[]{:S(2)}) collective-permute-start(f32[1,2,1,128,128]{3,4,2,1,0:T(8,128)S(1)} %get-tuple-element.169), channel_id=1, source_target_pairs={{0,1},{2,3},{4,5},{6,7},{8,9},{10,11},{12,13},{14,15},{16,17},{18,... | collective-permute-start | bytes 393224 | tf_op jit(solution)/shard_map/ppermute | solution.py:23
  37.4 181.0 %collective-permute-start.5 = (f32[1,2,1,128,128]{3,4,2,1,0:T(8,128)}, f32[1,2,1,128,128]{3,4,2,1,0:T(8,128)S(1)}, u32[]{:S(2)}, u32[]{:S(2)}) collective-permute-start(f32[1,2,1,128,128]{3,4,2,1,0:T(8,128)} %get-tuple-element.166), channel_id=1, source_target_pairs={{1,0},{3,2},{5,4},{7,6},{9,8},{11,10},{13,12},{15,14},{17,16},{19,... | collective-permute-start | bytes 393224 | tf_op jit(solution)/shard_map/ppermute | solution.py:24
  38.7 179.7 %collective-permute-start.6 = (f32[1,2,1,128,128]{3,4,2,1,0:T(8,128)}, f32[1,2,1,128,128]{3,4,2,1,0:T(8,128)S(1)}, u32[]{:S(2)}, u32[]{:S(2)}) collective-permute-start(f32[1,2,1,128,128]{3,4,2,1,0:T(8,128)} %get-tuple-element.167), channel_id=1, source_target_pairs={{0,1},{2,3},{4,5},{6,7},{8,9},{10,11},{12,13},{14,15},{16,17},{18,... | collective-permute-start | bytes 393224 | tf_op jit(solution)/shard_map/ppermute | solution.py:23
  279.4 2.4 copy-start.2
  342.7 1.6 copy-start
  344.3 1.6 copy-start.1
  354.7 10.9 %copy-start.4 = (u32[32]{0:T(128)S(1)}, u32[32]{0:T(128)}, u32[]{:S(2)}) copy-start(u32[32]{0:T(128)} %constant.162) | copy-start | bytes 388
  354.7 9.1 %all-to-all-start = ((f32[2,5,2,2,2048]{4,3,2,1,0:T(2,128)}), f32[2,5,2,2,2048]{4,3,2,1,0:T(2,128)S(1)}, u32[]{:S(2)}, u32[]{:S(2)}) async-start(f32[2,5,2,2,2048]{4,3,2,1,0:T(2,128)} %pad_maximum_fusion.14), calls=%async_computation | async-start | bytes 655360 | tf_op jit(solution)/shard_map/all_to_all | solution.py:122
  358.3 55.9 %all-gather.2.cloned.1.call-start = ((), (), s32[]{:S(2)}) async-start(), calls=%async_computation.2 | async-start | bytes 1114112 | tf_op jit(solution)/shard_map/all_gather | solution.py:37
  448.3 9.3 %all-to-all-start.1 = ((f32[2,2,8,2048]{3,1,0,2:T(2,128)}), f32[2,2,8,2048]{3,1,0,2:T(2,128)S(1)}, u32[]{:S(2)}, u32[]{:S(2)}) async-start(f32[2,2,8,2048]{3,1,0,2:T(2,128)} %copy.36), calls=%async_computation.1 | async-start | bytes 524288 | tf_op jit(solution)/shard_map/all_to_all | solution.py:167
Sparse Core Ops, SparseCore 0:
  365.8 48.3 all-gather.1
